TPU v7x, 256 devices: a whole 4x4x8 slice. The times are simulated.
256 devices in a mesh: ctx: 64 (over y, z, core), head: 4 (over x).
Axes of the slice: x: 4, y: 4, z: 8, core: 2. Of those that a mesh axis runs over, the one named last changes fastest.
Arguments:
- queries: bfloat16 [65536, 4096], P('ctx', 'head'), may hold values from -6.4 to 6.4
- keys: bfloat16 [65536, 4096], P('ctx', 'head'), may hold values from -0.62 to 0.62
- values: bfloat16 [65536, 4096], P('ctx', 'head'), may hold values from -7.6 to 7.6
- log_decay: float32 [32, 65536], P('head', 'ctx'), may hold values from -1.6 to 0, as said below
- gain: float32 [4096], P('head'), may hold values from 0.1 to 1.9
Outputs:
- shift: float32 [4096], P('head')
- covariance: float32 [4096, 2048], P(('head', 'ctx'))
Inputs may be any that keep to these rules, and one draw needn't show every extreme that they name: log_decay is negative everywhere.
All inputs are finite; a program needn't handle non-finite values.
Results may differ from a plain program's by a relative error of at most 0.0045.
The roundings to bfloat16 on the way count: a program that leaves them out, or rounds other values in their place, can miss the bound.
Values may be sent and summed in bfloat16 or wider, within the bound.
A program may use at most 128 MiB of HBM per device.

v0:
```python
import jax
import jax.numpy as jnp
from jax import lax
from jax.sharding import PartitionSpec as P

HEAD_DIM = 128
SPAN = 256


def entering(value, axis, join, neutral):
    count, mine = (lax.axis_size(axis), lax.axis_index(axis))
    pieces = jax.tree.map(lambda part: lax.all_gather(part, axis), value)
    total = jax.tree.map(
        lambda part, zero: jnp.full_like(part, 0) + jnp.asarray(zero, part.dtype), value, neutral
    )

    def turn(position, total):
        longer = join(total, jax.tree.map(lambda part: part[position], pieces))
        return jax.tree.map(lambda new, old: jnp.where(position < mine, new, old), longer, total)

    return lax.fori_loop(0, count - 1, turn, total)


def merged(value, axis, join):
    pieces = jax.tree.map(lambda part: lax.all_gather(part, axis), value)
    head = jax.tree.map(lambda part: part[0], pieces)
    tail = jax.tree.map(lambda part: part[1:], pieces)
    total, _ = lax.scan(lambda total, slab: (join(total, slab), None), head, tail)
    return total


def from_partner(value, axis, apart):
    mask = 2**apart
    pairs = [(source, source ^ mask) for source in range(lax.axis_size(axis))]
    return lax.ppermute(value, axis, pairs)


def block_step(state, inputs):
    query, key, value, decay = inputs
    cumul = jnp.cumsum(decay, axis=1)
    scores = jnp.einsum("thd,shd->hts", query, key, preferred_element_type=jnp.float32)
    length = query.shape[0]
    later = jnp.arange(length)[:, None] >= jnp.arange(length)[None, :]
    diff = cumul[:, :, None] - cumul[:, None, :]
    factor = jnp.where(later[None], jnp.exp(jnp.where(later[None], diff, 0.0)), 0.0)
    weights = (scores * factor).astype(jnp.bfloat16)
    inner = jnp.einsum("hts,shd->thd", weights, value, preferred_element_type=jnp.float32)
    scaled_q = query.astype(jnp.float32) * jnp.exp(cumul).T[:, :, None]
    outer = jnp.einsum("thd,hde->the", scaled_q, state, precision=lax.Precision.HIGHEST)
    scaled_k = key.astype(jnp.float32) * jnp.exp(cumul[:, -1:] - cumul).T[:, :, None]
    update = jnp.einsum(
        "shd,she->hde", scaled_k, value.astype(jnp.float32), precision=lax.Precision.HIGHEST
    )
    new_state = jnp.exp(cumul[:, -1])[:, None, None] * state + update
    return (new_state, inner + outer)


def run_blocks(start, query, key, value, decay):
    count, heads, size = query.shape
    blocks = count // SPAN
    shaped = (
        query.reshape(blocks, SPAN, heads, size),
        key.reshape(blocks, SPAN, heads, size),
        value.reshape(blocks, SPAN, heads, size),
        decay.reshape(heads, blocks, SPAN).transpose(1, 0, 2),
    )
    ending, raw = lax.scan(block_step, start, shaped)
    return (ending, raw.reshape(count, heads, size))


def chain_join(earlier, later):
    return (earlier[0] * later[0], later[0][:, None, None] * earlier[1] + later[1])


def incoming_state(total, ending):
    heads = total.shape[0]
    identity = (jnp.ones((heads,), jnp.float32), jnp.zeros_like(ending))
    carried = entering((total, ending), "ctx", chain_join, identity)
    return carried[1]


def extreme_join(first, second):
    return (jnp.maximum(first[0], second[0]), jnp.minimum(first[1], second[1]))


def body(queries, keys, values, log_decay, gain):
    count, width = queries.shape
    heads = width // HEAD_DIM
    query = queries.reshape(count, heads, HEAD_DIM)
    key = keys.reshape(count, heads, HEAD_DIM)
    value = values.reshape(count, heads, HEAD_DIM)
    cumul = jnp.cumsum(log_decay, axis=1)
    total = jnp.exp(cumul[:, -1])
    scaled_k = key.astype(jnp.float32) * jnp.exp(cumul[:, -1:] - cumul).T[:, :, None]
    ending = jnp.einsum(
        "shd,she->hde", scaled_k, value.astype(jnp.float32), precision=lax.Precision.HIGHEST
    )
    arrived = incoming_state(total, ending)
    _, raw = run_blocks(arrived, query, key, value, log_decay)
    scale = jnp.sqrt(jnp.mean(raw * raw, axis=-1, keepdims=True) + 1e-06)
    attended = (
        (raw / scale * gain.reshape(heads, HEAD_DIM)).reshape(count, width).astype(jnp.bfloat16)
    )
    top, bottom = merged(
        (jnp.max(attended, axis=0), jnp.min(attended, axis=0)), "ctx", extreme_join
    )
    shift = (top.astype(jnp.float32) + bottom.astype(jnp.float32)) / 2.0
    partner = from_partner(attended, "head", 0)
    own_means = jnp.mean(attended.astype(jnp.float32), axis=0)
    other_means = jnp.mean(partner.astype(jnp.float32), axis=0)
    own_centered = (attended.astype(jnp.float32) - own_means).astype(jnp.bfloat16)
    other_centered = (partner.astype(jnp.float32) - other_means).astype(jnp.bfloat16)
    parity = lax.axis_index("head") % 2
    lower = parity == 0
    pair_data = jnp.concatenate(
        [
            jnp.where(lower, own_centered, other_centered),
            jnp.where(lower, other_centered, own_centered),
        ],
        axis=1,
    )
    pair_means = jnp.concatenate(
        [jnp.where(lower, own_means, other_means), jnp.where(lower, other_means, own_means)]
    )
    offset = parity * width
    shards = lax.axis_size("ctx")
    rows = width // shards
    first_row = lax.axis_index("ctx") * rows
    every_mean = lax.all_gather(pair_means[None, :], "ctx", axis=0, tiled=True)
    channel_spread = every_mean - jnp.mean(every_mean, axis=0)
    spread_rows = lax.dynamic_slice_in_dim(channel_spread, offset + first_row, rows, 1)
    fix = count * jnp.dot(spread_rows.T, channel_spread, precision=lax.Precision.HIGHEST)
    gram = lax.psum_scatter(
        lax.dot_general(
            own_centered, pair_data, (((0,), (0,)), ((), ())), preferred_element_type=jnp.float32
        ),
        "ctx",
        scatter_dimension=0,
        tiled=True,
    )
    covariance = (gram + fix) / (count * shards)
    return (shift, covariance)


def solution(mesh):
    placed = (P("ctx", "head"), P("ctx", "head"), P("ctx", "head"), P("head", "ctx"), P("head"))
    return jax.shard_map(
        body,
        mesh=mesh,
        in_specs=placed,
        out_specs=(P("head"), P(("head", "ctx"), None)),
        check_vma=False,
    )
```

profile of v0, /device:TPU:2, one launch (start us, length us, event | category | flops | bytes accessed | tf_op | source)
XLA Modules:
  0.0 510.4 jit_solution(9900833300421825028)
XLA Ops:
  8.0 2.3 reduce-window.14
  10.9 4.1 copy.83
  15.0 6.1 %fusion.24 = f32[8,128,128]{2,1,0:T(8,128)} fusion(f32[1024,8,128]{0,2,1:T(8,128)} %bitcast.142, f32[1024,8]{0,1:T(8,128)S(1)} %exponential_bitcast_fusion.2, bf16[1024,1024]{1,0:T(8,128)(2,1)} %param.13), kind=kOutput, calls=%fused_computation.51 | convolution fusion | flops 1611661312 | bytes 6848512 | tf_op jit(solution)/shard_map/shd,she->hde/dot_general | solution.py:95
  22.7 136.0 %all-reduce = f32[512]{0:T(512)S(1)} all-reduce(f32[512]{0:T(512)S(1)} %bitcast_dynamic-update-slice_fusion), channel_id=2, replica_groups=mesh['ctx'=64,'head'=4] {'ctx'}, use_global_device_ids=true, to_apply=%add | all-reduce | flops 512 | bytes 4096
  158.8 1.9 copy.92
  160.8 1.9 copy.93
  162.7 2.0 copy.94
  164.7 2.1 all-gather.7.cloned.1.call-done
  166.7 76.4 %while.40 = (s32[]{:T(128)}, f32[8,128,128]{2,1,0:T(8,128)S(1)}, s32[]{:T(128)}, f32[64,8]{1,0:T(8,128)S(1)}, f32[64,8,128,128]{3,2,1,0:T(8,128)}, /*index=5*/s32[]{:T(128)}, s32[]{:T(128)}) while((s32[]{:T(128)}, f32[8,128,128]{2,1,0:T(8,128)S(1)}, s32[]{:T(128)}, f32[64,8]{1,0:T(8,128)S(1)}, f32[64,8,128,128]{3,2,1,0:T(8,128)}, ...), condition=%wide.region_3.4_spmd.clone, body=%wide.region_2.3_spmd.clone.sunk | while | flops 524292 | bytes 1573065 | solution.py:21
  168.0 1.2 fusion.45
  169.2 1.2 fusion.45
  172.8 1.2 fusion.45
  174.0 1.2 fusion.45
  175.2 1.2 fusion.45
  178.9 1.2 fusion.45
  180.1 1.2 fusion.45
  243.2 36.9 %while.38 = (s32[]{:T(128)}, f32[8,128,128]{2,1,0:T(8,128)S(1)}, f32[4,256,8,128]{1,3,2,0:T(8,128)}, f32[4,8,256]{2,1,0:T(8,128)}, bf16[4,256,8,128]{3,2,1,0:T(8...) while((s32[]{:T(128)}, f32[8,128,128]{2,1,0:T(8,128)S(1)}, ...), condition=%wide.region_7.8_spmd, body=%wide.region_4.7_spmd.sunk | while | flops 1078265856 | bytes 11248913 | solution.py:67
  244.7 1.3 constant_dynamic-slice_fusion.6
  246.0 1.4 convolution_bitcast_fusion.2
  248.5 2.0 fusion.44
  250.8 1.6 convolution_add_fusion.2
  254.0 1.3 constant_dynamic-slice_fusion.6
  255.2 1.4 convolution_bitcast_fusion.2
  257.7 2.0 fusion.44
  260.0 1.6 convolution_add_fusion.2
  263.2 1.3 constant_dynamic-slice_fusion.6
  264.5 1.4 convolution_bitcast_fusion.2
  267.0 2.0 fusion.44
  269.3 1.6 convolution_add_fusion.2
  272.4 1.3 constant_dynamic-slice_fusion.6
  273.7 1.4 convolution_bitcast_fusion.2
  276.2 2.0 fusion.44
  278.5 1.6 convolution_add_fusion.2
  280.1 2.6 multiply_reduce_fusion
  282.7 5.3 %copy.78 = f32[4,256,8,128]{3,2,1,0:T(8,128)} copy(f32[4,256,8,128]{1,3,2,0:T(8,128)} %get-tuple-element.162) | data formatting | bytes 8388608 | tf_op jit(solution)/shard_map/while | solution.py:67
  290.4 2.2 fusion.19
  293.4 4.2 convert_reduce_fusion.1
  297.6 43.2 %collective-permute-done = bf16[1024,1024]{1,0:T(8,128)(2,1)} collective-permute-done((bf16[1024,1024]{1,0:T(8,128)(2,1)S(1)}, bf16[1024,1024]{1,0:T(8,128)(2,1)}, u32[]{:S(2)}, u32[]{:S(2)}) %collective-permute-start) | collective-permute-done | bytes 2097184 | tf_op jit(solution)/shard_map/ppermute | solution.py:35
  340.7 2.0 convert_reduce_fusion
  342.7 2.8 broadcast_select_fusion.1
  345.5 7.0 %fusion.20 = f32[1024,2048]{1,0:T(8,128)} fusion(bf16[1024,1024]{1,0:T(8,128)(2,1)S(1)} %get-tuple-element.263, bf16[1024,1024]{1,0:T(8,128)(2,1)S(1)} %get-tuple-element.262, bf16[1024,1024]{1,0:T(8,128)(2,1)S(1)} %fusion.19, f32[1024]{0:T(1024)S(1)} %multiply_bitcast_fusion), kind=kOutput, calls=%fused_computation.43 | convolution fusion | flops 4306501632 | bytes 14684160 | tf_op jit(solution)/shard_map/dot_general | solution.py:134
  352.5 1.6 copy-done.3
  354.9 42.3 %all-gather.4 = bf16[64,1,1024]{2,1,0:T(2,128)(2,1)S(1)} all-gather(bf16[1,1,1024]{2,1,0:T(2,128)(2,1)S(1)} %reshape.171), channel_id=1, replica_groups=mesh['ctx'=64,'head'=4] {'ctx'}, dimensions={0}, use_global_device_ids=true | all-gather | bytes 133120 | tf_op jit(solution)/shard_map/all_gather | solution.py:25
  397.5 43.1 %all-gather.3 = bf16[64,1,1024]{2,1,0:T(2,128)(2,1)S(1)} all-gather(bf16[1,1,1024]{2,1,0:T(2,128)(2,1)S(1)} %reshape.169), channel_id=1, replica_groups=mesh['ctx'=64,'head'=4] {'ctx'}, dimensions={0}, use_global_device_ids=true | all-gather | bytes 133120 | tf_op jit(solution)/shard_map/all_gather | solution.py:25
  441.0 5.5 %while.39 = (s32[]{:T(128)}, bf16[1024]{0:T(1024)(128)(2,1)S(1)}, bf16[1024]{0:T(1024)(128)(2,1)S(1)}, bf16[63,1024]{1,0:T(8,128)(2,1)S(1)}, bf16[63,1024]{1,0:T(8,128)(2,1)S(1)}, /*index=5*/s32[]{:T(128)}) while((s32[]{:T(128)}, bf16[1024]{0:T(1024)(128)(2,1)S(1)}, bf16[1024]{0:T(1024)(128)(2,1)S(1)}, bf16[63,1024]{1,0:T(8,128)(2,1)S(1)}, ...), condition=%wide.region_12.13_spmd, body=%wide.region_11.12_spmd.sunk | while | flops 2050 | bytes 20553 | solution.py:28
  447.1 48.6 %all-gather.2 = f32[131072]{0:T(1024)S(1)} all-gather(f32[2048]{0:T(1024)S(1)} %pad_maximum_fusion), channel_id=4, replica_groups=mesh['ctx'=64,'head'=4] {'ctx'}, dimensions={0}, use_global_device_ids=true | all-gather | bytes 532480 | tf_op jit(solution)/shard_map/all_gather | solution.py:129
  496.3 5.7 %reduce-scatter.2.cloned.1.call-done = f32[16,2048]{1,0:T(8,128)} async-done(((f32[1024,2048]{1,0:T(8,128)}), f32[16,2048]{1,0:T(8,128)}) %reduce-scatter.2.cloned.1.call-update) | async-done | bytes 131088 | tf_op jit(solution)/shard_map/reduce_scatter | solution.py:133
  502.0 1.6 add_multiply_fusion
  (405 shorter events, 90.7 us)
Async XLA Ops:
  7.2 159.6 %all-gather.7.cloned.1.call-start = ((), (), s32[]{:S(2)}) async-start(), calls=%async_computation.2 | async-start | bytes 34078720 | tf_op jit(solution)/shard_map/all_gather | solution.py:12
  15.0 6.3 %copy-start.6 = (u32[256]{0:T(256)S(1)}, u32[256]{0:T(256)}, u32[]{:S(2)}) copy-start(u32[256]{0:T(256)} %constant.110) | copy-start | bytes 3076
  15.0 143.8 %copy-start.1 = (bf16[1024,1024]{1,0:T(8,128)(2,1)S(1)}, bf16[1024,1024]{1,0:T(8,128)(2,1)}, u32[]{:S(2)}) copy-start(bf16[1024,1024]{1,0:T(8,128)(2,1)} %param.12) | copy-start | bytes 6291460
  21.2 480.8 %reduce-scatter.2.cloned.1.call-start = ((), (), s32[]{:S(2)}) async-start(), calls=%async_computation.1 | async-start | bytes 8519680 | tf_op jit(solution)/shard_map/reduce_scatter | solution.py:133
  158.8 2.0 copy-start.2
  158.8 3.9 copy-start.4
  287.9 1.4 copy-start.5
  288.2 2.2 copy-start
  292.5 48.2 %collective-permute-start = (bf16[1024,1024]{1,0:T(8,128)(2,1)S(1)}, bf16[1024,1024]{1,0:T(8,128)(2,1)}, u32[]{:S(2)}, u32[]{:S(2)}) collective-permute-start(bf16[1024,1024]{1,0:T(8,128)(2,1)S(1)} %fusion.19), channel_id=1, source_target_pairs={{0,1},{1,0},{2,3},{3,2},{4,5},{5,4},{6,7},{7,6},{8,9},{9,8},{10,11... | collective-permute-start | bytes 6291464 | tf_op jit(solution)/shard_map/ppermute | solution.py:35
  352.5 1.6 copy-start.3
Sparse Core Ops, SparseCore 0:
  21.3 145.3 all-gather.6
  352.6 149.3 reduce-scatter.1
where the time goes:
time: 514 us; the launch traced here: 510 us
  blocking collectives  270 us (53%)
  other arithmetic  98.1 us (19%)
  waiting for transfers between devices  51 us (10%)
  local copies, waits for them, and re-layouts  38.8 us (8%)
  matrix products  33.5 us (7%)
  between operations  14.9 us (3%)
    unnamed x1, blocking collectives  136 us
    all_gather x2, blocking collectives, merged(): pieces = jax.tree.map(lambda part: lax.all_gather(part, axis), value)  85.3 us
    select_n x63, other arithmetic, turn(): jnp.where(position < mine, new, old)  73.9 us
    all_gather x1, blocking collectives, body(): every_mean = lax.all_gather(pair_means[None, :], 'ctx', axis=0, tiled=True)  48.6 us
    ppermute x1, waiting for transfers between devices, from_partner(): return lax.ppermute(value, axis, pairs)  43.2 us
  transfers between devices with their start and end apart: 3, of which 3 were waited for; matrix products, arithmetic and copies ran while one was open for 4% of the time, Pallas kernels for 0%

commit v1 on v0

--- a/solution.py
+++ b/solution.py
@@ -126,7 +126,9 @@
     shards = lax.axis_size("ctx")
     rows = width // shards
     first_row = lax.axis_index("ctx") * rows
-    every_mean = lax.all_gather(pair_means[None, :], "ctx", axis=0, tiled=True)
+    every_mean = jnp.concatenate(
+        lax.all_to_all(jnp.stack([pair_means[None, :]] * lax.axis_size("ctx")), "ctx", 0, 0), axis=0
+    )
     channel_spread = every_mean - jnp.mean(every_mean, axis=0)
     spread_rows = lax.dynamic_slice_in_dim(channel_spread, offset + first_row, rows, 1)
     fix = count * jnp.dot(spread_rows.T, channel_spread, precision=lax.Precision.HIGHEST)

time: 514 us -> 514 us (level)
  blocking collectives: 270 us -> 229 us
  waiting for transfers between devices: 51 us -> 86 us
  starting transfers between devices: 0.95 us -> 6.96 us
    all_gather x1 -> x0, blocking collectives: 48.6 us -> none  [body(): every_mean = lax.all_gather(pair_means[None, :], 'ctx', axis=0, tiled=True)]
    reduce_scatter x1, waiting for transfers between devices: 5.7 us -> 40.8 us  [body(): lax.psum_scatter(lax.dot_general(own_centered, pair_data, (((0,), (0,)),...]
    all_gather x2, blocking collectives: 85.3 us -> 92.8 us  [merged(): pieces = jax.tree.map(lambda part: lax.all_gather(part, axis), value)]
    all_to_all x0 -> x1, starting transfers between devices: none -> 6.01 us  [body(): lax.all_to_all(jnp.stack([pair_means[None, :]] * lax.axis_size('ctx')), '...]
  transfers between devices with their start and end apart: 3 -> 4, of which waited for: 3 -> 3; matrix products, arithmetic and copies ran while one was open for 4% -> 4% of each run, Pallas kernels for 0% -> 0%
where the time goes in v1:
time: 514 us; the launch traced here: 510 us
  blocking collectives  229 us (45%)
  other arithmetic  98.5 us (19%)
  waiting for transfers between devices  86 us (17%)
  local copies, waits for them, and re-layouts  38.2 us (7%)
  matrix products  33.5 us (7%)
  between operations  14.9 us (3%)
  starting transfers between devices  6.96 us (1%)
    unnamed x1, blocking collectives  136 us
    all_gather x2, blocking collectives, merged(): pieces = jax.tree.map(lambda part: lax.all_gather(part, axis), value)  92.8 us
    select_n x63, other arithmetic, turn(): jnp.where(position < mine, new, old)  73.9 us
    ppermute x1, waiting for transfers between devices, from_partner(): return lax.ppermute(value, axis, pairs)  43.2 us
    reduce_scatter x1, waiting for transfers between devices, body(): lax.psum_scatter(lax.dot_general(own_centered, pair_data, (((0,), (0,)),...  40.8 us
  transfers between devices with their start and end apart: 4, of which 3 were waited for; matrix products, arithmetic and copies ran while one was open for 4% of the time, Pallas kernels for 0%

profile of v1, /device:TPU:2, one launch (start us, length us, event | category | flops | bytes accessed | tf_op | source)
XLA Modules:
  0.0 510.3 jit_solution(13979369654597585410)
XLA Ops:
  8.0 2.3 reduce-window.14
  10.9 4.1 copy.98
  15.0 6.1 %fusion.24 = f32[8,128,128]{2,1,0:T(8,128)} fusion(f32[1024,8,128]{0,2,1:T(8,128)} %bitcast.144, f32[1024,8]{0,1:T(8,128)S(1)} %exponential_bitcast_fusion.2, bf16[1024,1024]{1,0:T(8,128)(2,1)} %param.13), kind=kOutput, calls=%fused_computation.51 | convolution fusion | flops 1611661312 | bytes 6848512 | tf_op jit(solution)/shard_map/shd,she->hde/dot_general | solution.py:95
  22.7 136.0 %all-reduce = f32[512]{0:T(512)S(1)} all-reduce(f32[512]{0:T(512)S(1)} %bitcast_dynamic-update-slice_fusion), channel_id=2, replica_groups=mesh['ctx'=64,'head'=4] {'ctx'}, use_global_device_ids=true, to_apply=%add | all-reduce | flops 512 | bytes 4096
  158.8 1.9 copy.109
  160.8 1.9 copy.110
  162.7 2.0 copy.111
  164.7 2.1 all-gather.6.cloned.1.call-done
  166.7 76.4 %while.40 = (s32[]{:T(128)}, f32[8,128,128]{2,1,0:T(8,128)S(1)}, s32[]{:T(128)}, f32[64,8]{1,0:T(8,128)S(1)}, f32[64,8,128,128]{3,2,1,0:T(8,128)}, /*index=5*/s32[]{:T(128)}, s32[]{:T(128)}) while((s32[]{:T(128)}, f32[8,128,128]{2,1,0:T(8,128)S(1)}, s32[]{:T(128)}, f32[64,8]{1,0:T(8,128)S(1)}, f32[64,8,128,128]{3,2,1,0:T(8,128)}, ...), condition=%wide.region_3.4_spmd.clone, body=%wide.region_2.3_spmd.clone.sunk | while | flops 524292 | bytes 1573065 | solution.py:21
  168.0 1.2 fusion.45
  169.2 1.2 fusion.45
  172.8 1.2 fusion.45
  174.0 1.2 fusion.45
  175.2 1.2 fusion.45
  178.9 1.2 fusion.45
  180.1 1.2 fusion.45
  183.7 1.2 fusion.45
  243.2 36.9 %while.38 = (s32[]{:T(128)}, f32[8,128,128]{2,1,0:T(8,128)S(1)}, f32[4,256,8,128]{1,3,2,0:T(8,128)}, f32[4,8,256]{2,1,0:T(8,128)}, bf16[4,256,8,128]{3,2,1,0:T(8...) while((s32[]{:T(128)}, f32[8,128,128]{2,1,0:T(8,128)S(1)}, ...), condition=%wide.region_7.8_spmd, body=%wide.region_4.7_spmd.sunk | while | flops 1078265856 | bytes 11248913 | solution.py:67
  244.7 1.3 constant_dynamic-slice_fusion.6
  246.0 1.4 convolution_bitcast_fusion.2
  248.5 2.0 fusion.44
  250.8 1.6 convolution_add_fusion.2
  254.0 1.3 constant_dynamic-slice_fusion.6
  255.2 1.4 convolution_bitcast_fusion.2
  257.7 2.0 fusion.44
  260.0 1.6 convolution_add_fusion.2
  263.2 1.3 constant_dynamic-slice_fusion.6
  264.5 1.4 convolution_bitcast_fusion.2
  267.0 2.0 fusion.44
  269.3 1.6 convolution_add_fusion.2
  272.4 1.3 constant_dynamic-slice_fusion.6
  273.7 1.4 convolution_bitcast_fusion.2
  276.2 2.0 fusion.44
  278.5 1.6 convolution_add_fusion.2
  280.1 2.6 multiply_reduce_fusion
  282.7 5.3 %copy.92 = f32[4,256,8,128]{3,2,1,0:T(8,128)} copy(f32[4,256,8,128]{1,3,2,0:T(8,128)} %get-tuple-element.162) | data formatting | bytes 8388608 | tf_op jit(solution)/shard_map/while | solution.py:67
  290.4 2.2 fusion.19
  293.4 4.2 convert_reduce_fusion.1
  297.6 43.2 %collective-permute-done = bf16[1024,1024]{1,0:T(8,128)(2,1)} collective-permute-done((bf16[1024,1024]{1,0:T(8,128)(2,1)S(1)}, bf16[1024,1024]{1,0:T(8,128)(2,1)}, u32[]{:S(2)}, u32[]{:S(2)}) %collective-permute-start) | collective-permute-done | bytes 2097184 | tf_op jit(solution)/shard_map/ppermute | solution.py:35
  340.7 2.0 convert_reduce_fusion
  342.7 2.8 broadcast_select_fusion.1
  345.5 7.0 %fusion.20 = f32[1024,2048]{1,0:T(8,128)} fusion(bf16[1024,1024]{1,0:T(8,128)(2,1)S(1)} %get-tuple-element.270, bf16[1024,1024]{1,0:T(8,128)(2,1)S(1)} %get-tuple-element.269, bf16[1024,1024]{1,0:T(8,128)(2,1)S(1)} %fusion.19, f32[1024]{0:T(1024)S(1)} %multiply_bitcast_fusion), kind=kOutput, calls=%fused_computation.43 | convolution fusion | flops 4306501632 | bytes 14684160 | tf_op jit(solution)/shard_map/dot_general | solution.py:136
  353.6 6.0 %all-to-all-start = ((f32[64,1,2048]{2,1,0:T(1,128)}), f32[64,1,2048]{2,1,0:T(1,128)S(1)}, u32[]{:S(2)}, u32[]{:S(2)}) async-start(f32[64,1,2048]{2,1,0:T(1,128)} %stack.3), calls=%async_computation.1 | async-start | bytes 1048576 | tf_op jit(solution)/shard_map/all_to_all | solution.py:130
  360.5 49.1 %all-gather.3 = bf16[64,1,1024]{2,1,0:T(2,128)(2,1)S(1)} all-gather(bf16[1,1,1024]{2,1,0:T(2,128)(2,1)S(1)} %reshape.176), channel_id=1, replica_groups=mesh['ctx'=64,'head'=4] {'ctx'}, dimensions={0}, use_global_device_ids=true | all-gather | bytes 133120 | tf_op jit(solution)/shard_map/all_gather | solution.py:25
  410.0 43.7 %all-gather.2 = bf16[64,1,1024]{2,1,0:T(2,128)(2,1)S(1)} all-gather(bf16[1,1,1024]{2,1,0:T(2,128)(2,1)S(1)} %reshape.174), channel_id=1, replica_groups=mesh['ctx'=64,'head'=4] {'ctx'}, dimensions={0}, use_global_device_ids=true | all-gather | bytes 133120 | tf_op jit(solution)/shard_map/all_gather | solution.py:25
  454.1 5.5 %while.39 = (s32[]{:T(128)}, bf16[1024]{0:T(1024)(128)(2,1)S(1)}, bf16[1024]{0:T(1024)(128)(2,1)S(1)}, bf16[63,1024]{1,0:T(8,128)(2,1)S(1)}, bf16[63,1024]{1,0:T(8,128)(2,1)S(1)}, /*index=5*/s32[]{:T(128)}) while((s32[]{:T(128)}, bf16[1024]{0:T(1024)(128)(2,1)S(1)}, bf16[1024]{0:T(1024)(128)(2,1)S(1)}, bf16[63,1024]{1,0:T(8,128)(2,1)S(1)}, ...), condition=%wide.region_12.13_spmd, body=%wide.region_11.12_spmd.sunk | while | flops 2050 | bytes 20553 | solution.py:28
  461.1 40.8 %reduce-scatter.2.cloned.1.call-done = f32[16,2048]{1,0:T(8,128)} async-done(((f32[1024,2048]{1,0:T(8,128)}), f32[16,2048]{1,0:T(8,128)}) %reduce-scatter.2.cloned.1.call-update) | async-done | bytes 131088 | tf_op jit(solution)/shard_map/reduce_scatter | solution.py:135
  501.9 1.6 add_multiply_fusion
  (406 shorter events, 91.0 us)
Async XLA Ops:
  7.2 159.6 %all-gather.6.cloned.1.call-start = ((), (), s32[]{:S(2)}) async-start(), calls=%async_computation.3 | async-start | bytes 34078720 | tf_op jit(solution)/shard_map/all_gather | solution.py:12
  15.0 6.3 %copy-start.6 = (u32[256]{0:T(256)S(1)}, u32[256]{0:T(256)}, u32[]{:S(2)}) copy-start(u32[256]{0:T(256)} %constant.110) | copy-start | bytes 3076
  15.0 143.8 %copy-start.1 = (bf16[1024,1024]{1,0:T(8,128)(2,1)S(1)}, bf16[1024,1024]{1,0:T(8,128)(2,1)}, u32[]{:S(2)}) copy-start(bf16[1024,1024]{1,0:T(8,128)(2,1)} %param.12) | copy-start | bytes 6291460
  21.2 480.7 %reduce-scatter.2.cloned.1.call-start = ((), (), s32[]{:S(2)}) async-start(), calls=%async_computation.2 | async-start | bytes 8519680 | tf_op jit(solution)/shard_map/reduce_scatter | solution.py:135
  158.8 2.0 copy-start.2
  158.8 3.9 copy-start.4
  287.9 1.4 copy-start.5
  288.2 2.2 copy-start
  292.5 48.2 %collective-permute-start = (bf16[1024,1024]{1,0:T(8,128)(2,1)S(1)}, bf16[1024,1024]{1,0:T(8,128)(2,1)}, u32[]{:S(2)}, u32[]{:S(2)}) collective-permute-start(bf16[1024,1024]{1,0:T(8,128)(2,1)S(1)} %fusion.19), channel_id=1, source_target_pairs={{0,1},{1,0},{2,3},{3,2},{4,5},{5,4},{6,7},{7,6},{8,9},{9,8},{10,11... | collective-permute-start | bytes 6291464 | tf_op jit(solution)/shard_map/ppermute | solution.py:35
  352.5 7.2 %copy-start.3 = (bf16[4,256,8,128]{1,3,2,0:T(8,128)(2,1)S(1)}, bf16[4,256,8,128]{1,3,2,0:T(8,128)(2,1)}, u32[]{:S(2)}) copy-start(bf16[4,256,8,128]{1,3,2,0:T(8,128)(2,1)} %get-tuple-element.264) | copy-start | bytes 6291460
  353.6 106.6 %all-to-all-start = ((f32[64,1,2048]{2,1,0:T(1,128)}), f32[64,1,2048]{2,1,0:T(1,128)S(1)}, u32[]{:S(2)}, u32[]{:S(2)}) async-start(f32[64,1,2048]{2,1,0:T(1,128)} %stack.3), calls=%async_computation.1 | async-start | bytes 1048576 | tf_op jit(solution)/shard_map/all_to_all | solution.py:130
Sparse Core Ops, SparseCore 0:
  21.3 145.3 all-gather.5
  352.6 149.2 reduce-scatter.1
